TPU v7x, 256 devices: a whole 4x4x8 slice. The times are simulated.
256 devices in a mesh: sub: 64 (over y_lo, z, x), blk: 4 (over y_hi, core).
Axes of the slice: x: 4, y: 4 (y_hi: 2, y_lo: 2; y = y_hi * 2 + y_lo), z: 8, core: 2. Of those that a mesh axis runs over, the one named last changes fastest.
Arguments:
- residual: float32 [32, 131072], P(None, ('sub', 'blk')), may hold values from -6 to 6
- fine_inverse: float32 [64, 2560, 2048], P('sub', None, 'blk'), may hold values from -1 to 1.1
- coarse_inverse: float32 [16384, 4, 4096], P('sub', 'blk'), may hold values from -0.5 to 0.5, as said below
- wanted_rows: int32 [64, 2, 256], P('sub'), may hold values from 0 to 2047
- wanted_count: int32 [64, 2], P('sub'), may hold values from 32 to 256, as said below
- aggregate: int32 [131072], P(('sub', 'blk')), may hold values from 0 to 255
Outputs:
- preconditioned: float32 [32, 131072], P(None, ('sub', 'blk'))
Inputs may be any that keep to these rules, and one draw needn't show every extreme that they name: M of the steps is symmetric: coarse_inverse[i, b, s * 64 + q] equals coarse_inverse[s * 256 + b * 64 + q, b2, s2 * 64 + q2] where i = s2 * 256 + b2 * 64 + q2. `wanted_count`: counts vary from side to side; in every draw some subdomain other than the first and last takes exactly 256 rows from one side.
All inputs are finite; a program needn't handle non-finite values.
Results may differ from a plain program's by a relative error of at most 0.000052.
Values sent between devices are 32-bit elements; how exact they have to be, the bound alone decides.
A program may use at most 64 MiB of HBM per device.

v0:
```python
import jax
import jax.numpy as jnp
from jax import lax
from jax.sharding import PartitionSpec as P


def with_halo(cells, sides, width):
    for axis, dim in sides:
        count = lax.axis_size(axis)
        ends = count - 1
        head = lax.slice_in_dim(cells, 0, width, axis=dim)
        tail = lax.slice_in_dim(cells, cells.shape[dim] - width, cells.shape[dim], axis=dim)
        cells = jnp.concatenate(
            [
                lax.ppermute(tail, axis, [(i, (i + 1) % count) for i in range(ends)]),
                cells,
                lax.ppermute(head, axis, [((i + 1) % count, i) for i in range(ends)]),
            ],
            axis=dim,
        )
    return cells


def mask_slots(picked, wanted_total):
    slot_ids = lax.broadcasted_iota(jnp.int32, (1, picked.shape[1]), 1)
    return jnp.where(slot_ids < wanted_total, picked, jnp.zeros_like(picked))


def on_device(residual, fine_inverse, coarse_inverse, wanted_rows, wanted_count, aggregate):
    own_block = lax.all_gather(residual, "blk", axis=1, tiled=True)
    own_len = own_block.shape[1]
    beside = with_halo(own_block, (("sub", 1),), own_len)
    left_raw = jnp.take(beside[:, :own_len], wanted_rows[0, 0], axis=1)
    right_raw = jnp.take(beside[:, 2 * own_len :], wanted_rows[0, 1], axis=1)
    left_halo = mask_slots(left_raw, wanted_count[0, 0])
    right_halo = mask_slots(right_raw, wanted_count[0, 1])
    extended = jnp.concatenate([left_halo, own_block, right_halo], axis=1)
    fine_part = jnp.dot(
        extended,
        fine_inverse[0],
        precision=lax.Precision.HIGHEST,
        preferred_element_type=jnp.float32,
    )
    coarse_table = coarse_inverse[:, 0, :]
    coarse_len = coarse_table.shape[0]
    levels = lax.broadcasted_iota(jnp.int32, (1, coarse_len), 1)
    onehot = (aggregate[:, None] == levels).astype(jnp.float32)
    partial_value = jnp.dot(
        residual, onehot, precision=lax.Precision.HIGHEST, preferred_element_type=jnp.float32
    )
    coarse_share = lax.psum_scatter(partial_value, "blk", scatter_dimension=1, tiled=True)
    partial_solution = lax.dot_general(
        lax.all_gather(coarse_share, "sub", axis=1, tiled=True),
        coarse_table,
        (((1,), (1,)), ((), ())),
        precision=lax.Precision.HIGHEST,
        preferred_element_type=jnp.float32,
    )
    coarse_solution = lax.psum(partial_solution, "blk")
    lifted = lax.dot_general(
        coarse_solution,
        onehot,
        (((1,), (1,)), ((), ())),
        precision=lax.Precision.HIGHEST,
        preferred_element_type=jnp.float32,
    )
    return fine_part + lifted


def solution(mesh):
    in_specs = (
        P(None, ("sub", "blk")),
        P("sub", None, "blk"),
        P("sub", "blk", None),
        P("sub", None, None),
        P("sub", None),
        P(("sub", "blk")),
    )
    out_specs = P(None, ("sub", "blk"))
    return jax.shard_map(
        on_device, mesh=mesh, in_specs=in_specs, out_specs=out_specs, check_vma=False
    )
```

profile of v0, /device:TPU:1, one launch (start us, length us, event | category | flops | bytes accessed | tf_op | source)
XLA Modules:
  0.0 259.5 jit_solution(2096369147131564380)
XLA Ops:
  6.5 10.5 %all_gather.6 = f32[32,2048]{1,0:T(8,128)S(1)} all-gather(f32[32,512]{1,0:T(8,128)} %param.8), channel_id=1, replica_groups=mesh['sub'=64,'blk'=4] {'blk'}, dimensions={1}, use_global_device_ids=true | all-gather | bytes 327680 | tf_op jit(solution)/shard_map/all_gather | solution.py:30
  17.1 1.3 collective-permute-start.1
  18.3 4.0 %collective-permute-start = (f32[32,2048]{1,0:T(8,128)S(1)}, f32[32,2048]{1,0:T(8,128)S(1)}, u32[]{:S(2)}, u32[]{:S(2)}) collective-permute-start(f32[32,2048]{1,0:T(8,128)S(1)} %all_gather.6), channel_id=1, source_target_pairs={{0,4},{4,8},{8,12},{12,16},{16,20},{20,24},{24,28},{28,32},{32,36}... | collective-permute-start | bytes 786440 | tf_op jit(solution)/shard_map/ppermute | solution.py:15
  22.4 1.2 convolution_bitcast_fusion
  23.6 0.8 copy.15
  24.3 0.8 fusion.17
  25.1 1.3 fusion.18
  26.5 0.6 compare_and_fusion
  27.1 0.7 compare_and_fusion.1
  27.8 31.8 %reduce-scatter.4.cloned.1.call-done = f32[64,32]{1,0:T(8,128)} async-done(((f32[256,32]{1,0:T(8,128)}), f32[64,32]{1,0:T(8,128)}) %reduce-scatter.4.cloned.1.call-update) | async-done | bytes 8208
  59.6 0.8 copy.16
  60.4 133.4 %all-gather = f32[64,64,32]{1,2,0:T(8,128)S(1)} all-gather(f32[1,64,32]{1,2,0:T(8,128)S(1)} %bitcast.29), channel_id=1, replica_groups=mesh['sub'=64,'blk'=4] {'sub'}, dimensions={0}, use_global_device_ids=true | all-gather | bytes 532480 | tf_op jit(solution)/shard_map/all_gather | solution.py:53
  193.8 0.6 copy.14
  194.4 0.4 reshape.35
  194.8 7.4 %fusion.2 = f32[32,256]{1,0:T(8,128)S(1)} fusion(f32[4096,32]{0,1:T(8,128)S(1)} %reshape.35, f32[256,1,4096]{2,1,0:T(1,128)} %param.10), kind=kOutput, calls=%fused_computation.4 | convolution fusion | flops 402653184 | bytes 4751360 | tf_op jit(solution)/shard_map/dot_general | solution.py:52
  202.1 41.3 %psum.7 = f32[32,256]{1,0:T(8,128)S(1)} all-reduce(f32[32,256]{1,0:T(8,128)S(1)} %fusion.2), channel_id=1, replica_groups=mesh['sub'=64,'blk'=4] {'blk'}, use_global_device_ids=true, to_apply=%region_1.3 | all-reduce | flops 8192 | bytes 65536 | tf_op jit(solution)/shard_map/psum | solution.py:59
  243.5 0.4 fusion.8
  243.9 0.3 copy.11
  244.3 0.7 gather_fusion.1
  245.0 0.1 bitcast_select_fusion
  245.2 0.3 copy.10
  245.5 0.7 gather_fusion
  246.3 0.1 bitcast_select_fusion.1
  246.5 6.2 %fusion.5 = f32[32,512]{1,0:T(8,128)} fusion(f32[32,512]{1,0:T(8,128)S(1)} %fusion.8, f32[1,2560,512]{2,1,0:T(8,128)} %param.9, f32[32,256]{1,0:T(8,128)S(1)} %copy.13, f32[32,2048]{1,0:T(8,128)S(1)} %all_gather.6, f32[32,256]{1,0:T(8,128)S(1)} %copy.12), kind=kOutput, calls=%fused_computation.7 | convolution fusion | flops 503496704 | bytes 5701632 | tf_op jit(solution)/shard_map/dot_general | solution.py:38
  (12 shorter events, 0.2 us)
Async XLA Ops:
  6.5 53.0 %reduce-scatter.4.cloned.1.call-start = ((), (), s32[]{:S(2)}) async-start(), calls=%async_computation.1 | async-start | bytes 163840
  17.1 226.9 %collective-permute-start.1 = (f32[32,2048]{1,0:T(8,128)S(1)}, f32[32,2048]{1,0:T(8,128)S(1)}, u32[]{:S(2)}, u32[]{:S(2)}) collective-permute-start(f32[32,2048]{1,0:T(8,128)S(1)} %all_gather.6), channel_id=1, source_target_pairs={{4,0},{8,4},{12,8},{16,12},{20,16},{24,20},{28,24},{32,28},{36,32}... | collective-permute-start | bytes 786440 | tf_op jit(solution)/shard_map/ppermute | solution.py:17
  18.3 226.9 %collective-permute-start = (f32[32,2048]{1,0:T(8,128)S(1)}, f32[32,2048]{1,0:T(8,128)S(1)}, u32[]{:S(2)}, u32[]{:S(2)}) collective-permute-start(f32[32,2048]{1,0:T(8,128)S(1)} %all_gather.6), channel_id=1, source_target_pairs={{0,4},{4,8},{8,12},{12,16},{16,20},{20,24},{24,28},{28,32},{32,36}... | collective-permute-start | bytes 786440 | tf_op jit(solution)/shard_map/ppermute | solution.py:15
  193.8 49.7 %copy-start = (s32[512]{0:T(512)S(1)}, s32[512]{0:T(512)}, u32[]{:S(2)}) copy-start(s32[512]{0:T(512)} %param.13) | copy-start | bytes 6148
Sparse Core Ops, SparseCore 0:
  24.5 35.0 reduce-scatter.3
where the time goes:
time: 260 us
  blocking collectives  185 us (71%)
  waiting for transfers between devices  31.8 us (12%)
  matrix products  15.2 us (6%)
  between operations  13.5 us (5%)
  local copies, waits for them, and re-layouts  6.92 us (3%)
  starting transfers between devices  5.29 us (2%)
    all_gather x1, blocking collectives, on_device(): lax.all_gather(coarse_share, 'sub', axis=1, tiled=True)  133 us
    psum x1, blocking collectives, on_device(): coarse_solution = lax.psum(partial_solution, 'blk')  41.3 us
    unnamed x2, waiting for transfers between devices  31.8 us
    all_gather x1, blocking collectives, on_device(): own_block = lax.all_gather(residual, 'blk', axis=1, tiled=True)  10.5 us
    dot_general x1, matrix products, on_device(): lax.dot_general(lax.all_gather(coarse_share, 'sub', axis=1, tiled=True),...  7.38 us
    dot_general x1, matrix products, on_device(): jnp.dot(extended, fine_inverse[0], precision=lax.Precision.HIGHEST, prefe...  6.2 us
  transfers between devices with their start and end apart: 3, of which 1 were waited for; matrix products, arithmetic and copies ran while one was open for 6% of the time, Pallas kernels for 0%

commit v1 on v0

--- a/solution.py
+++ b/solution.py
@@ -50,7 +50,9 @@
     )
     coarse_share = lax.psum_scatter(partial_value, "blk", scatter_dimension=1, tiled=True)
     partial_solution = lax.dot_general(
-        lax.all_gather(coarse_share, "sub", axis=1, tiled=True),
+        jnp.concatenate(
+            lax.all_to_all(jnp.stack([coarse_share] * lax.axis_size("sub")), "sub", 0, 0), axis=1
+        ),
         coarse_table,
         (((1,), (1,)), ((), ())),
         precision=lax.Precision.HIGHEST,

time: 260 us -> 128 us (0.49)
  blocking collectives: 185 us -> 26.5 us
  waiting for transfers between devices: 31.8 us -> 44.6 us
  starting transfers between devices: 5.29 us -> 15.5 us
    all_gather x1 -> x0, blocking collectives: 133 us -> none  [on_device(): lax.all_gather(coarse_share, 'sub', axis=1, tiled=True)]
    psum x1, blocking collectives: 41.3 us -> 15.9 us  [on_device(): coarse_solution = lax.psum(partial_solution, 'blk')]
    all_to_all x0 -> x1, waiting for transfers between devices: none -> 12 us  [on_device(): lax.all_to_all(jnp.stack([coarse_share] * lax.axis_size('sub')), 'sub', 0...]
    all_to_all x0 -> x1, starting transfers between devices: none -> 10.2 us  [on_device(): lax.all_to_all(jnp.stack([coarse_share] * lax.axis_size('sub')), 'sub', 0...]
  transfers between devices with their start and end apart: 3 -> 4, of which waited for: 1 -> 2; matrix products, arithmetic and copies ran while one was open for 6% -> 8% of each run, Pallas kernels for 0% -> 0%
where the time goes in v1:
time: 128 us
  waiting for transfers between devices  44.6 us (35%)
  blocking collectives  26.5 us (21%)
  starting transfers between devices  15.5 us (12%)
  matrix products  15.2 us (12%)
  between operations  13.6 us (11%)
  local copies, waits for them, and re-layouts  9.38 us (7%)
  other arithmetic  3.39 us (3%)
    unnamed x2, waiting for transfers between devices  32.6 us
    psum x1, blocking collectives, on_device(): coarse_solution = lax.psum(partial_solution, 'blk')  15.9 us
    all_to_all x1, waiting for transfers between devices, on_device(): lax.all_to_all(jnp.stack([coarse_share] * lax.axis_size('sub')), 'sub', 0...  12 us
    all_gather x1, blocking collectives, on_device(): own_block = lax.all_gather(residual, 'blk', axis=1, tiled=True)  10.5 us
    all_to_all x1, starting transfers between devices, on_device(): lax.all_to_all(jnp.stack([coarse_share] * lax.axis_size('sub')), 'sub', 0...  10.2 us
    dot_general x1, matrix products, on_device(): lax.dot_general(jnp.concatenate(lax.all_to_all(jnp.stack([coarse_share] *...  7.38 us
    dot_general x1, matrix products, on_device(): jnp.dot(extended, fine_inverse[0], precision=lax.Precision.HIGHEST, prefe...  6.21 us
    ppermute x1, starting transfers between devices, with_halo(): lax.ppermute(tail, axis, [(i, (i + 1) % count) for i in range(ends)])  4 us
  transfers between devices with their start and end apart: 4, of which 2 were waited for; matrix products, arithmetic and copies ran while one was open for 8% of the time, Pallas kernels for 0%

profile of v1, /device:TPU:1, one launch (start us, length us, event | category | flops | bytes accessed | tf_op | source)
XLA Modules:
  0.0 128.0 jit_solution(6531148949822479992)
XLA Ops:
  6.5 10.5 %all_gather.3 = f32[32,2048]{1,0:T(8,128)S(1)} all-gather(f32[32,512]{1,0:T(8,128)} %param.8), channel_id=1, replica_groups=mesh['sub'=64,'blk'=4] {'blk'}, dimensions={1}, use_global_device_ids=true | all-gather | bytes 327680 | tf_op jit(solution)/shard_map/all_gather | solution.py:30
  17.1 1.3 %collective-permute-start.1 = (f32[32,2048]{1,0:T(8,128)S(1)}, f32[32,2048]{1,0:T(8,128)S(1)}, u32[]{:S(2)}, u32[]{:S(2)}) collective-permute-start(f32[32,2048]{1,0:T(8,128)S(1)} %all_gather.3), channel_id=1, source_target_pairs={{4,0},{8,4},{12,8},{16,12},{20,16},{24,20},{28,24},{32,28},{36,32}... | collective-permute-start | bytes 786440 | tf_op jit(solution)/shard_map/ppermute | solution.py:17
  18.3 4.0 %collective-permute-start = (f32[32,2048]{1,0:T(8,128)S(1)}, f32[32,2048]{1,0:T(8,128)S(1)}, u32[]{:S(2)}, u32[]{:S(2)}) collective-permute-start(f32[32,2048]{1,0:T(8,128)S(1)} %all_gather.3), channel_id=1, source_target_pairs={{0,4},{4,8},{8,12},{12,16},{16,20},{20,24},{24,28},{28,32},{32,36}... | collective-permute-start | bytes 786440 | tf_op jit(solution)/shard_map/ppermute | solution.py:15
  22.4 1.2 convolution_bitcast_fusion
  23.6 0.7 copy.14
  24.3 0.8 fusion.17
  25.1 1.3 %fusion.18 = (s32[1,1]{1,0:T(1,128)}, s32[1,1]{1,0:T(1,128)}) fusion(s32[1,2]{1,0:T(1,128)} %param.12), kind=kLoop, calls=%fused_computation.30 | loop fusion | bytes 16 | tf_op jit(solution)/shard_map/slice | solution.py:35
  26.4 0.6 compare_and_fusion
  27.0 32.6 %reduce-scatter.4.cloned.1.call-done = f32[64,32]{1,0:T(8,128)} async-done(((f32[256,32]{1,0:T(8,128)}), f32[64,32]{1,0:T(8,128)}) %reduce-scatter.4.cloned.1.call-update) | async-done | bytes 8208
  59.6 0.8 copy.15
  60.5 1.4 %reshape.50 = f32[64,1,2048]{2,1,0:T(1,128)} reshape(f32[64,32,64]{2,1,0:T(8,128)S(1)} %stack.2) | data formatting | bytes 1048576
  62.0 10.2 %all-to-all-start = ((f32[64,1,2048]{2,1,0:T(1,128)}), f32[64,1,2048]{2,1,0:T(1,128)S(1)}, u32[]{:S(2)}, u32[]{:S(2)}) async-start(f32[64,1,2048]{2,1,0:T(1,128)} %reshape.50), calls=%async_computation | async-start | bytes 1048576 | tf_op jit(solution)/shard_map/all_to_all | solution.py:54
  72.1 0.7 compare_and_fusion.1
  73.2 0.7 gather_fusion.1
  74.5 0.7 gather_fusion
  75.4 12.0 %all-to-all-done = f32[64,1,2048]{2,1,0:T(1,128)S(1)} async-done(((f32[64,1,2048]{2,1,0:T(1,128)}), f32[64,1,2048]{2,1,0:T(1,128)S(1)}, u32[]{:S(2)}, u32[]{:S(2)}) %all-to-all-start) | async-done | bytes 524320 | tf_op jit(solution)/shard_map/all_to_all | solution.py:54
  87.4 0.5 broadcast.44
  87.9 1.9 %reduce = f32[64,2048]{1,0:T(8,128)S(1)} reduce(f32[64,1,2048]{2,1,0:T(1,128)S(1)} %all-to-all-done, f32[]{:T(128)} %broadcast.44), dimensions={1}, to_apply=%all_to_all.3.reduce_sub_computation | reduce | bytes 1048580 | tf_op jit(solution)/shard_map/all_to_all | solution.py:54
  89.8 0.4 reshape.51
  90.2 0.6 copy.13
  91.2 7.4 %fusion.2 = f32[32,256]{1,0:T(8,128)S(1)} fusion(f32[32,4096]{1,0:T(8,128)S(1)} %reshape.25, f32[256,1,4096]{2,1,0:T(1,128)} %param.10), kind=kOutput, calls=%fused_computation.4 | convolution fusion | flops 402653184 | bytes 4751360 | tf_op jit(solution)/shard_map/dot_general | solution.py:52
  98.6 15.9 %psum.7 = f32[32,256]{1,0:T(8,128)S(1)} all-reduce(f32[32,256]{1,0:T(8,128)S(1)} %fusion.2), channel_id=1, replica_groups=mesh['sub'=64,'blk'=4] {'blk'}, use_global_device_ids=true, to_apply=%region_1.3 | all-reduce | flops 8192 | bytes 65536 | tf_op jit(solution)/shard_map/psum | solution.py:61
  114.6 0.4 fusion.8
  114.9 6.2 %fusion.5 = f32[32,512]{1,0:T(8,128)} fusion(f32[32,512]{1,0:T(8,128)S(1)} %fusion.8, f32[1,2560,512]{2,1,0:T(8,128)} %param.9, f32[32,256]{1,0:T(8,128)S(1)} %copy.12, f32[32,2048]{1,0:T(8,128)S(1)} %all_gather.3, f32[32,256]{1,0:T(8,128)S(1)} %copy.11), kind=kOutput, calls=%fused_computation.7 | convolution fusion | flops 503496704 | bytes 5701632 | tf_op jit(solution)/shard_map/dot_general | solution.py:38
  (18 shorter events, 1.6 us)
Async XLA Ops:
  6.5 53.0 %reduce-scatter.4.cloned.1.call-start = ((), (), s32[]{:S(2)}) async-start(), calls=%async_computation.2 | async-start | bytes 163840
  17.1 55.8 %collective-permute-start.1 = (f32[32,2048]{1,0:T(8,128)S(1)}, f32[32,2048]{1,0:T(8,128)S(1)}, u32[]{:S(2)}, u32[]{:S(2)}) collective-permute-start(f32[32,2048]{1,0:T(8,128)S(1)} %all_gather.3), channel_id=1, source_target_pairs={{4,0},{8,4},{12,8},{16,12},{20,16},{24,20},{28,24},{32,28},{36,32}... | collective-permute-start | bytes 786440 | tf_op jit(solution)/shard_map/ppermute | solution.py:17
  18.3 55.8 %collective-permute-start = (f32[32,2048]{1,0:T(8,128)S(1)}, f32[32,2048]{1,0:T(8,128)S(1)}, u32[]{:S(2)}, u32[]{:S(2)}) collective-permute-start(f32[32,2048]{1,0:T(8,128)S(1)} %all_gather.3), channel_id=1, source_target_pairs={{0,4},{4,8},{8,12},{12,16},{16,20},{20,24},{24,28},{28,32},{32,36}... | collective-permute-start | bytes 786440 | tf_op jit(solution)/shard_map/ppermute | solution.py:15
  62.0 25.4 %all-to-all-start = ((f32[64,1,2048]{2,1,0:T(1,128)}), f32[64,1,2048]{2,1,0:T(1,128)S(1)}, u32[]{:S(2)}, u32[]{:S(2)}) async-start(f32[64,1,2048]{2,1,0:T(1,128)} %reshape.50), calls=%async_computation | async-start | bytes 1048576 | tf_op jit(solution)/shard_map/all_to_all | solution.py:54
  90.2 24.3 %copy-start = (s32[512]{0:T(512)S(1)}, s32[512]{0:T(512)}, u32[]{:S(2)}) copy-start(s32[512]{0:T(512)} %param.13) | copy-start | bytes 6148
Sparse Core Ops, SparseCore 0:
  24.4 35.0 reduce-scatter.3

commit v2 on v0

--- a/solution.py
+++ b/solution.py
@@ -56,7 +56,7 @@
         precision=lax.Precision.HIGHEST,
         preferred_element_type=jnp.float32,
     )
-    coarse_solution = lax.psum(partial_solution, "blk")
+    coarse_solution = jnp.sum(lax.all_gather(partial_solution, "blk"), axis=0)
     lifted = lax.dot_general(
         coarse_solution,
         onehot,

time: 260 us -> 254 us (0.977)
  blocking collectives: 185 us -> 180 us
    psum x1 -> x0, blocking collectives: 41.3 us -> none  [on_device(): coarse_solution = lax.psum(partial_solution, 'blk')]
    all_gather x0 -> x1, blocking collectives: none -> 35.6 us  [on_device(): coarse_solution = jnp.sum(lax.all_gather(partial_solution, 'blk'), axis=0)]
where the time goes in v2:
time: 254 us
  blocking collectives  180 us (71%)
  waiting for transfers between devices  31.8 us (13%)
  matrix products  15.2 us (6%)
  between operations  13.5 us (5%)
  local copies, waits for them, and re-layouts  6.92 us (3%)
  starting transfers between devices  5.29 us (2%)
    all_gather x1, blocking collectives, on_device(): lax.all_gather(coarse_share, 'sub', axis=1, tiled=True)  133 us
    all_gather x1, blocking collectives, on_device(): coarse_solution = jnp.sum(lax.all_gather(partial_solution, 'blk'), axis=0)  35.6 us
    unnamed x2, waiting for transfers between devices  31.8 us
    all_gather x1, blocking collectives, on_device(): own_block = lax.all_gather(residual, 'blk', axis=1, tiled=True)  10.5 us
    dot_general x1, matrix products, on_device(): lax.dot_general(lax.all_gather(coarse_share, 'sub', axis=1, tiled=True),...  7.38 us
    dot_general x1, matrix products, on_device(): jnp.dot(extended, fine_inverse[0], precision=lax.Precision.HIGHEST, prefe...  6.2 us
  transfers between devices with their start and end apart: 3, of which 1 were waited for; matrix products, arithmetic and copies ran while one was open for 6% of the time, Pallas kernels for 0%

profile of v2, /device:TPU:1, one launch (start us, length us, event | category | flops | bytes accessed | tf_op | source)
XLA Modules:
  0.0 253.8 jit_solution(8287578799915773218)
XLA Ops:
  6.5 10.5 %all_gather.12 = f32[32,2048]{1,0:T(8,128)S(1)} all-gather(f32[32,512]{1,0:T(8,128)} %param.8), channel_id=1, replica_groups=mesh['sub'=64,'blk'=4] {'blk'}, dimensions={1}, use_global_device_ids=true | all-gather | bytes 327680 | tf_op jit(solution)/shard_map/all_gather | solution.py:30
  17.1 1.3 collective-permute-start.1
  18.3 4.0 %collective-permute-start = (f32[32,2048]{1,0:T(8,128)S(1)}, f32[32,2048]{1,0:T(8,128)S(1)}, u32[]{:S(2)}, u32[]{:S(2)}) collective-permute-start(f32[32,2048]{1,0:T(8,128)S(1)} %all_gather.12), channel_id=1, source_target_pairs={{0,4},{4,8},{8,12},{12,16},{16,20},{20,24},{24,28},{28,32},{32,36}... | collective-permute-start | bytes 786440 | tf_op jit(solution)/shard_map/ppermute | solution.py:15
  22.4 1.2 convolution_bitcast_fusion
  23.6 0.8 copy.15
  24.3 0.8 fusion.17
  25.1 1.3 fusion.18
  26.5 0.6 compare_and_fusion
  27.1 0.7 compare_and_fusion.1
  27.8 31.8 %reduce-scatter.4.cloned.1.call-done = f32[64,32]{1,0:T(8,128)} async-done(((f32[256,32]{1,0:T(8,128)}), f32[64,32]{1,0:T(8,128)}) %reduce-scatter.4.cloned.1.call-update) | async-done | bytes 8208
  59.6 0.8 copy.16
  60.4 133.4 %all-gather.1 = f32[64,64,32]{1,2,0:T(8,128)S(1)} all-gather(f32[1,64,32]{1,2,0:T(8,128)S(1)} %bitcast.31), channel_id=1, replica_groups=mesh['sub'=64,'blk'=4] {'sub'}, dimensions={0}, use_global_device_ids=true | all-gather | bytes 532480 | tf_op jit(solution)/shard_map/all_gather | solution.py:53
  193.8 0.6 copy.14
  194.4 0.4 reshape.36
  194.8 7.4 %fusion.2 = f32[32,256]{1,0:T(8,128)S(1)} fusion(f32[4096,32]{0,1:T(8,128)S(1)} %reshape.36, f32[256,1,4096]{2,1,0:T(1,128)} %param.10), kind=kOutput, calls=%fused_computation.4 | convolution fusion | flops 402653184 | bytes 4751360 | tf_op jit(solution)/shard_map/dot_general | solution.py:52
  202.1 35.6 %all-gather = f32[128,256]{1,0:T(8,128)S(1)} all-gather(f32[32,256]{1,0:T(8,128)S(1)} %fusion.2), channel_id=2, replica_groups=mesh['sub'=64,'blk'=4] {'blk'}, dimensions={0}, use_global_device_ids=true | all-gather | bytes 163840 | tf_op jit(solution)/shard_map/all_gather | solution.py:59
  237.8 0.4 fusion.8
  238.2 0.3 copy.11
  238.5 0.7 gather_fusion.1
  239.3 0.1 bitcast_select_fusion
  239.5 0.3 copy.10
  239.8 0.7 gather_fusion
  240.6 0.1 bitcast_select_fusion.1
  240.8 6.2 %fusion.5 = f32[32,512]{1,0:T(8,128)} fusion(f32[32,512]{1,0:T(8,128)S(1)} %fusion.8, f32[1,2560,512]{2,1,0:T(8,128)} %param.9, f32[32,256]{1,0:T(8,128)S(1)} %copy.13, f32[32,2048]{1,0:T(8,128)S(1)} %all_gather.12, f32[32,256]{1,0:T(8,128)S(1)} %copy.12), kind=kOutput, calls=%fused_computation.7 | convolution fusion | flops 503496704 | bytes 5701632 | tf_op jit(solution)/shard_map/dot_general | solution.py:38
  (13 shorter events, 0.2 us)
Async XLA Ops:
  6.5 53.0 %reduce-scatter.4.cloned.1.call-start = ((), (), s32[]{:S(2)}) async-start(), calls=%async_computation.1 | async-start | bytes 163840
  17.1 221.1 %collective-permute-start.1 = (f32[32,2048]{1,0:T(8,128)S(1)}, f32[32,2048]{1,0:T(8,128)S(1)}, u32[]{:S(2)}, u32[]{:S(2)}) collective-permute-start(f32[32,2048]{1,0:T(8,128)S(1)} %all_gather.12), channel_id=1, source_target_pairs={{4,0},{8,4},{12,8},{16,12},{20,16},{24,20},{28,24},{32,28},{36,32}... | collective-permute-start | bytes 786440 | tf_op jit(solution)/shard_map/ppermute | solution.py:17
  18.3 221.1 %collective-permute-start = (f32[32,2048]{1,0:T(8,128)S(1)}, f32[32,2048]{1,0:T(8,128)S(1)}, u32[]{:S(2)}, u32[]{:S(2)}) collective-permute-start(f32[32,2048]{1,0:T(8,128)S(1)} %all_gather.12), channel_id=1, source_target_pairs={{0,4},{4,8},{8,12},{12,16},{16,20},{20,24},{24,28},{28,32},{32,36}... | collective-permute-start | bytes 786440 | tf_op jit(solution)/shard_map/ppermute | solution.py:15
  193.8 44.0 %copy-start = (s32[512]{0:T(512)S(1)}, s32[512]{0:T(512)}, u32[]{:S(2)}) copy-start(s32[512]{0:T(512)} %param.13) | copy-start | bytes 6148
Sparse Core Ops, SparseCore 0:
  24.5 35.0 reduce-scatter.3
